TPU v7x, 256 devices: a whole 4x4x8 slice. The times are simulated.
256 devices in a mesh: batch: 4 (over y), lat: 8 (over x, core), lon: 8 (over z).
Axes of the slice: x: 4, y: 4, z: 8, core: 2. Of those that a mesh axis runs over, the one named last changes fastest.
Arguments:
- patches: bfloat16 [4, 16, 24, 128, 640], P('batch', 'lat', 'lon'), may hold values from -6 to 6
- kept_index: int32 [4, 16, 24, 64], P('batch', 'lat', 'lon'), may hold values from 0 to 127, as said below
- kept_count: int32 [4, 16, 24], P('batch', 'lat', 'lon'), may hold values from 32 to 64, as said below
- embed_weight: bfloat16 [640, 1280], P('batch'), may hold values from -0.25 to 0.25
- local_qkv: bfloat16 [1280, 3840], P('batch'), may hold values from -6 to 6
- local_out: bfloat16 [1280, 1280], P('batch'), may hold values from -0.15625 to 0.15625
- global_qkv: bfloat16 [1280, 3840], P('batch'), may hold values from -6 to 6
Outputs:
- mixed: bfloat16 [4, 16, 24, 64, 1280], P('batch', 'lat', 'lon')
Inputs may be any that keep to these rules, and one draw needn't show every extreme that they name: `kept_index`: in each window all 64 entries are distinct offsets; the first kept_count of them are the kept tokens in rising order. `kept_count`: every device holds, in its sample, a window with exactly 64 kept tokens.
All inputs are finite; a program needn't handle non-finite values.
Results may differ from a plain program's by a relative error of at most 0.023.
Values may be sent and summed in bfloat16 or wider, within the bound.
A program may use at most 128 MiB of HBM per device.

v0:
```python
import jax
import jax.numpy as jnp
from jax import lax
from jax.sharding import PartitionSpec as P

HEADS = 8
HD = 160
norm_eps = 1e-05
mask_floor = -1e30


def layer_norm(values):
    centre = values - jnp.mean(values, axis=-1, keepdims=True)
    spread = jnp.mean(centre * centre, axis=-1, keepdims=True)
    return centre * lax.rsqrt(spread + norm_eps)


def product(left_rows, right_rows):
    return jnp.dot(left_rows, right_rows, preferred_element_type=jnp.float32)


def gather_weight(shard):
    rows = shard.shape[0] // lax.axis_size("lat")
    piece = lax.dynamic_slice_in_dim(shard, lax.axis_index("lat") * rows, rows, 0)
    return lax.all_gather(piece, ("batch", "lat"), axis=0, tiled=True)


def attend(proj, keep_mask):
    groups, rows = proj.shape[:2]
    split = proj.reshape(groups, rows, 3, HEADS, HD)
    scores = jnp.einsum(
        "bnhd,bmhd->bhnm", split[:, :, 0], split[:, :, 1], preferred_element_type=jnp.float32
    ) * HD ** (-0.5)
    scores = jnp.where(keep_mask[:, None, None, :], scores, mask_floor)
    scores = scores - jnp.max(scores, axis=-1, keepdims=True)
    weights = jnp.exp(scores)
    probabilities = (weights / jnp.sum(weights, axis=-1, keepdims=True)).astype(jnp.bfloat16)
    blended = jnp.einsum(
        "bhnm,bmhd->bnhd", probabilities, split[:, :, 2], preferred_element_type=jnp.float32
    )
    return blended.astype(jnp.bfloat16).reshape(groups, rows, HEADS * HD)


def body(patches, kept_index, kept_count, embed_weight, local_qkv, local_out, global_qkv):
    lat_windows = patches.shape[1]
    lon_windows = patches.shape[2]
    windows = lat_windows * lon_windows
    tokens = patches.shape[3]
    most = kept_index.shape[3]
    rows = windows * most
    inner = HEADS * HD
    owners = lax.axis_size("lat") * lax.axis_size("lon")
    owned = tokens // owners
    me = lax.axis_index("lat") * lax.axis_size("lon") + lax.axis_index("lon")
    patch_rows = patches.reshape(windows, tokens, patches.shape[4])
    kept = lax.broadcasted_iota(jnp.int32, (windows, most), 1) < kept_count.reshape(windows, 1)
    marks = jnp.where(kept, kept_index.reshape(windows, most), -1)
    all_marks = lax.all_gather(marks, ("lat", "lon"), axis=0, tiled=True)
    wanted = me + owners * lax.broadcasted_iota(jnp.int32, (owned, 1, 1), 0)
    member = jnp.any(all_marks[None] == wanted, axis=-1)
    chosen = (
        marks[:, :, None] == lax.broadcasted_iota(jnp.int32, (windows, most, tokens), 2)
    ).astype(jnp.bfloat16)
    picked = (
        jnp.einsum("wkt,wtd->wkd", chosen, patch_rows, preferred_element_type=jnp.float32)
        .astype(jnp.bfloat16)
        .reshape(rows, -1)
    )
    embedded = product(picked, gather_weight(embed_weight)).astype(jnp.bfloat16)
    normed = layer_norm(embedded.astype(jnp.float32)).astype(jnp.bfloat16)
    local_proj = product(normed, gather_weight(local_qkv)).astype(jnp.bfloat16)
    local_mix = attend(local_proj.reshape(windows, most, -1), kept).reshape(rows, inner)
    hidden = (embedded.astype(jnp.float32) + product(local_mix, gather_weight(local_out))).astype(
        jnp.bfloat16
    )
    normed_global = layer_norm(hidden.astype(jnp.float32)).astype(jnp.bfloat16)
    slots = jnp.einsum(
        "wkt,wkd->twd",
        chosen,
        normed_global.reshape(windows, most, -1),
        preferred_element_type=jnp.float32,
    ).astype(jnp.bfloat16)
    received = lax.all_to_all(
        slots.reshape(owned, owners, windows, -1),
        ("lat", "lon"),
        split_axis=1,
        concat_axis=1,
        tiled=True,
    )
    group = owners * windows
    global_proj = product(received.reshape(owned * group, -1), gather_weight(global_qkv))
    blended = attend(
        global_proj.astype(jnp.bfloat16).reshape(owned, group, -1), member.reshape(owned, group)
    )
    returned = lax.all_to_all(
        blended.reshape(owned, owners, windows, inner),
        ("lat", "lon"),
        split_axis=1,
        concat_axis=1,
        tiled=True,
    ).reshape(tokens, windows, inner)
    result = jnp.einsum(
        "wkt,twd->wkd", chosen, returned, preferred_element_type=jnp.float32
    ).astype(jnp.bfloat16)
    return result.reshape(1, lat_windows, lon_windows, most, inner)


def solution(mesh):
    return jax.shard_map(
        body,
        mesh=mesh,
        in_specs=(
            P("batch", "lat", "lon", None, None),
            P("batch", "lat", "lon", None),
            P("batch", "lat", "lon"),
            P("batch", None),
            P("batch", None),
            P("batch", None),
            P("batch", None),
        ),
        out_specs=P("batch", "lat", "lon", None, None),
        check_vma=False,
    )
```

profile of v0, /device:TPU:1, one launch (start us, length us, event | category | flops | bytes accessed | tf_op | source)
XLA Modules:
  0.0 421.8 jit_solution(6911432130226525416)
XLA Ops:
  6.6 1.7 dynamic-slice_bitcast_fusion
  8.4 0.7 constant_dynamic-slice_fusion.2
  9.2 1.5 constant_dynamic-slice_fusion.1
  10.8 1.7 constant_dynamic-slice_fusion
  12.6 0.1 lt.26
  12.7 0.1 iota_compare_fusion.4
  12.8 0.3 convolution_convert_fusion.6
  13.2 49.4 %all-gather.13.cloned.1.call-done = bf16[32,20,1280]{2,1,0:T(8,128)(2,1)} async-done(((bf16[1,20,1280]{2,1,0:T(8,128)(2,1)}), bf16[32,20,1280]{2,1,0:T(8,128)(2,1)}) %all-gather.13.cloned.1.call-update) | async-done | bytes 1638416 | tf_op jit(solution)/shard_map/all_gather | solution.py:25
  62.6 2.5 reshape.115
  65.1 1.0 convert_reduce_fusion
  66.1 0.4 fusion.11
  66.5 59.2 %all-gather.7.cloned.1.call-done = bf16[1280,3840]{1,0:T(8,128)(2,1)} async-done(((bf16[40,3840]{1,0:T(8,128)(2,1)}), bf16[1280,3840]{1,0:T(8,128)(2,1)}) %all-gather.7.cloned.1.call-update) | async-done | bytes 9830416 | tf_op jit(solution)/shard_map/all_gather | solution.py:25
  125.7 9.4 %convolution_convert_fusion.1 = bf16[384,3840]{1,0:T(8,128)(2,1)} fusion(bf16[1280,3840]{1,0:T(8,128)(2,1)} %all-gather.7.cloned.1.call-done, bf16[384,1280]{1,0:T(8,128)(2,1)S(1)} %get-tuple-element.12, f32[384]{0:T(512)S(1)} %add_rsqrt_fusion.1, f32[384]{0:T(512)S(1)} %broadcast_multiply_fusion.1), kind=kOutput, calls=%fused_computation.7 | convolution fusion | flops 3778314240 | bytes 13765632 | tf_op jit(solution)/shard_map/dot_general | solution.py:19
  135.1 9.2 %reshape_reshape.12 = bf16[6,64,3,8,160]{4,3,2,1,0:T(8,128)(2,1)} reshape(bf16[384,3840]{1,0:T(8,128)(2,1)} %convolution_convert_fusion.1) | data formatting | bytes 5898240 | tf_op jit(solution)/shard_map/reshape;reshape | solution.py:30
  144.2 2.8 fusion.34
  147.0 0.8 multiply_select_fusion.4
  147.8 1.1 copy-done.6
  148.9 0.4 fusion.35
  149.3 4.0 fusion.21
  153.4 2.3 copy.51
  155.7 2.5 reshape_reshape.13
  158.2 19.7 %all-gather.9.cloned.1.call-done = bf16[1280,1280]{1,0:T(8,128)(2,1)} async-done(((bf16[40,1280]{1,0:T(8,128)(2,1)}), bf16[1280,1280]{1,0:T(8,128)(2,1)}) %all-gather.9.cloned.1.call-update) | async-done | bytes 3276816 | tf_op jit(solution)/shard_map/all_gather | solution.py:25
  177.9 3.8 fusion.36
  181.6 0.3 multiply_reduce_fusion
  182.0 0.3 multiply_convert_fusion
  182.3 0.8 convolution_convert_fusion.2
  183.1 3.3 copy.52
  186.4 9.6 %all-to-all-start = ((bf16[2,64,6,1280]{3,0,2,1:T(2,128)(2,1)}), bf16[2,64,6,1280]{3,0,2,1:T(2,128)(2,1)S(1)}, u32[]{:S(2)}, u32[]{:S(2)}) async-start(bf16[2,64,6,1280]{3,0,2,1:T(2,128)(2,1)} %copy.52), calls=%async_computation | async-start | bytes 3932160 | tf_op jit(solution)/shard_map/all_to_all | solution.py:83
  195.9 0.1 fusion.50
  196.0 83.2 %all-gather.1 = s32[64,6,64]{2,1,0:T(8,128)S(1)} all-gather(s32[1,6,64]{2,1,0:T(8,128)S(1)} %fusion.50), channel_id=1, replica_groups=mesh['batch'=4,'lat'=8,'lon'=8] {'lat','lon'}, dimensions={0}, use_global_device_ids=true | all-gather | bytes 99840 | tf_op jit(solution)/shard_map/all_gather | solution.py:58
  279.2 0.1 copy.56
  279.4 0.1 compare_reduce_fusion
  279.5 1.8 copy.53
  281.3 2.8 reshape.111
  284.1 13.2 %convolution_convert_fusion = bf16[768,3840]{1,0:T(8,128)(2,1)} fusion(bf16[768,1280]{1,0:T(8,128)(2,1)S(1)} %reshape.111, bf16[1280,3840]{1,0:T(8,128)(2,1)} %all-gather.11.cloned.1.call-done), kind=kOutput, calls=%fused_computation.6 | convolution fusion | flops 7552696320 | bytes 17694720 | tf_op jit(solution)/shard_map/dot_general | solution.py:19
  297.3 16.6 %reshape.118 = bf16[2,384,3,8,160]{4,3,2,1,0:T(8,128)(2,1)} reshape(bf16[768,3840]{1,0:T(8,128)(2,1)} %convolution_convert_fusion) | data formatting | bytes 11796480 | tf_op jit(solution)/shard_map/reshape;reshape | solution.py:30
  313.9 7.0 %fusion.33 = (bf16[2,384,1,8,160]{4,3,2,1,0:T(8,128)(2,1)}, bf16[2,384,1,8,160]{4,3,2,1,0:T(8,128)(2,1)}, bf16[2,384,1,8,160]{4,3,2,1,0:T(8,128)(2,1)}) fusion(bf16[2,384,3,8,160]{4,3,2,1,0:T(8,128)(2,1)} %reshape.118), kind=kLoop, calls=%fused_computation.64 | loop fusion | bytes 11796480 | tf_op jit(solution)/shard_map/slice | solution.py:39
  320.9 3.8 copy.70
  324.7 4.7 %copy.71 = bf16[2,384,1,8,160]{1,4,3,0,2:T(8,128)(2,1)} copy(bf16[2,384,1,8,160]{4,3,2,1,0:T(8,128)(2,1)} %get-tuple-element.7) | data formatting | bytes 3932160
  329.4 4.8 %copy.69 = bf16[2,384,1,8,160]{1,4,3,0,2:T(8,128)(2,1)} copy(bf16[2,384,1,8,160]{4,3,2,1,0:T(8,128)(2,1)} %get-tuple-element.5) | data formatting | bytes 3932160
  334.2 3.5 fusion.13
  337.7 4.1 fusion.37
  341.8 2.8 convert_bitcast_fusion
  344.6 5.0 %copy.60 = bf16[2,384,8,160]{3,2,0,1:T(8,128)(2,1)} copy(bf16[2,384,8,160]{1,3,2,0:T(8,128)(2,1)} %convert_bitcast_fusion) | data formatting | bytes 3932160 | tf_op jit(solution)/shard_map/convert_element_type | solution.py:41
  349.6 6.9 %reshape_reshape.15 = bf16[2,64,6,1280]{3,0,2,1:T(2,128)(2,1)S(1)} reshape(bf16[2,384,8,160]{3,2,0,1:T(8,128)(2,1)} %copy.60) | data formatting | bytes 3932160 | tf_op jit(solution)/shard_map/reshape;reshape | solution.py:96
  356.4 57.1 %all_to_all.10 = bf16[2,64,6,1280]{3,0,2,1:T(2,128)(2,1)S(1)} all-to-all(bf16[2,64,6,1280]{3,0,2,1:T(2,128)(2,1)S(1)} %reshape_reshape.15), channel_id=1, replica_groups=mesh['batch'=4,'lat'=8,'lon'=8] {'lat','lon'}, dimensions={1} | all-to-all | bytes 3932160 | tf_op jit(solution)/shard_map/all_to_all | solution.py:95
  413.6 0.2 copy.61
  413.8 1.4 convolution_convert_fusion.3
  (32 shorter events, 0.4 us)
Async XLA Ops:
  6.5 1.8 copy-start
  6.5 6.0 %copy-start.5 = (s32[1,2,3]{2,1,0:T(2,128)S(1)}, s32[1,2,3]{2,1,0:T(2,128)}, u32[]{:S(2)}) copy-start(s32[1,2,3]{2,1,0:T(2,128)} %param.9) | copy-start | bytes 76
  6.5 6.1 %copy-start.4 = (s32[1,2,3,64]{3,1,2,0:T(2,128)S(1)}, s32[1,2,3,64]{3,1,2,0:T(2,128)}, u32[]{:S(2)}) copy-start(s32[1,2,3,64]{3,1,2,0:T(2,128)} %param.8) | copy-start | bytes 4612
  6.5 6.3 %copy-start.3 = (bf16[1,2,3,128,640]{4,3,2,1,0:T(8,128)(2,1)S(1)}, bf16[1,2,3,128,640]{4,3,2,1,0:T(8,128)(2,1)}, u32[]{:S(2)}) copy-start(bf16[1,2,3,128,640]{4,3,2,1,0:T(8,128)(2,1)} %param.7) | copy-start | bytes 2949124
  6.5 56.1 %all-gather.13.cloned.1.call-start = ((), (), s32[]{:S(2)}) async-start(), calls=%async_computation.5 | async-start | bytes 2027520 | tf_op jit(solution)/shard_map/all_gather | solution.py:25
  8.3 117.4 %all-gather.7.cloned.1.call-start = ((), (), s32[]{:S(2)}) async-start(), calls=%async_computation.2 | async-start | bytes 10137600 | tf_op jit(solution)/shard_map/all_gather | solution.py:25
  9.1 168.7 %all-gather.9.cloned.1.call-start = ((), (), s32[]{:S(2)}) async-start(), calls=%async_computation.3 | async-start | bytes 3379200 | tf_op jit(solution)/shard_map/all_gather | solution.py:25
  10.8 273.3 %all-gather.11.cloned.1.call-start = ((), (), s32[]{:S(2)}) async-start(), calls=%async_computation.4 | async-start | bytes 10137600 | tf_op jit(solution)/shard_map/all_gather | solution.py:25
  147.8 1.1 copy-start.6
  186.4 93.1 %all-to-all-start = ((bf16[2,64,6,1280]{3,0,2,1:T(2,128)(2,1)}), bf16[2,64,6,1280]{3,0,2,1:T(2,128)(2,1)S(1)}, u32[]{:S(2)}, u32[]{:S(2)}) async-start(bf16[2,64,6,1280]{3,0,2,1:T(2,128)(2,1)} %copy.52), calls=%async_computation | async-start | bytes 3932160 | tf_op jit(solution)/shard_map/all_to_all | solution.py:83
  337.7 4.1 copy-start.2
  413.6 1.7 copy-start.1
Sparse Core Ops, SparseCore 0:
  10.0 52.6 all-gather.12
  65.2 60.4 all-gather.6
  128.3 49.5 all-gather.8
  180.4 74.4 all-gather.10
where the time goes:
time: 423 us; the launch traced here: 422 us
  blocking collectives  140 us (33%)
  waiting for transfers between devices  128 us (30%)
  local copies, waits for them, and re-layouts  83.2 us (20%)
  matrix products  40.9 us (10%)
  between operations  13.3 us (3%)
  starting transfers between devices  9.74 us (2%)
  other arithmetic  5.86 us (1%)
    all_gather x4, waiting for transfers between devices, gather_weight(): return lax.all_gather(piece, ('batch', 'lat'), axis=0, tiled=True)  128 us
    all_gather x1, blocking collectives, body(): all_marks = lax.all_gather(marks, ('lat', 'lon'), axis=0, tiled=True)  83.2 us
    all_to_all x1, blocking collectives, body(): lax.all_to_all(blended.reshape(owned, owners, windows, inner), ('lat', 'l...  57.1 us
    dot_general x4, matrix products, product(): return jnp.dot(left_rows, right_rows, preferred_element_type=jnp.float32)  27.4 us
    another operation x2, local copies, waits for them, and re-layouts, attend(): split = proj.reshape(groups, rows, 3, HEADS, HD)  25.8 us
    unnamed x22, local copies, waits for them, and re-layouts  18.8 us
    all_to_all x1, starting transfers between devices, body(): lax.all_to_all(slots.reshape(owned, owners, windows, -1), ('lat', 'lon'),...  9.58 us
  transfers between devices with their start and end apart: 5, of which 3 were waited for; matrix products, arithmetic and copies ran while one was open for 13% of the time, Pallas kernels for 0%

commit v1 on v0

--- a/solution.py
+++ b/solution.py
@@ -7,6 +7,11 @@
 HD = 160
 norm_eps = 1e-05
 mask_floor = -1e30
+
+
+def all_by_exchange(x, axis, d):
+    sent = jnp.stack([x] * lax.axis_size(axis))
+    return jnp.concatenate(lax.all_to_all(sent, axis, 0, 0), axis=d)
 
 
 def layer_norm(values):
@@ -22,7 +27,7 @@
 def gather_weight(shard):
     rows = shard.shape[0] // lax.axis_size("lat")
     piece = lax.dynamic_slice_in_dim(shard, lax.axis_index("lat") * rows, rows, 0)
-    return lax.all_gather(piece, ("batch", "lat"), axis=0, tiled=True)
+    return all_by_exchange(piece, ("batch", "lat"), 0)
 
 
 def attend(proj, keep_mask):

time: 423 us -> 592 us (1.40)
  blocking collectives: 140 us -> 209 us
  waiting for transfers between devices: 128 us -> 196 us
  starting transfers between devices: 9.74 us -> 43.8 us
  between operations: 13.3 us -> 0.24 us
  local copies, waits for them, and re-layouts: 83.2 us -> 92.6 us
    all_to_all x0 -> x4, waiting for transfers between devices: none -> 148 us  [all_by_exchange(): return jnp.concatenate(lax.all_to_all(sent, axis, 0, 0), axis=d)]
    all_gather x4 -> x0, waiting for transfers between devices: 128 us -> none  [gather_weight(): return lax.all_gather(piece, ('batch', 'lat'), axis=0, tiled=True)]
    all_gather x1, blocking collectives: 83.2 us -> 153 us  [body(): all_marks = lax.all_gather(marks, ('lat', 'lon'), axis=0, tiled=True)]
    all_to_all x1, waiting for transfers between devices: 0.01 us -> 48 us  [body(): lax.all_to_all(slots.reshape(owned, owners, windows, -1), ('lat', 'lon'),...]
    all_to_all x0 -> x4, starting transfers between devices: none -> 31.8 us  [all_by_exchange(): return jnp.concatenate(lax.all_to_all(sent, axis, 0, 0), axis=d)]
    another operation x0 -> x4, local copies, waits for them, and re-layouts: none -> 12.1 us  [all_by_exchange(): sent = jnp.stack([x] * lax.axis_size(axis))]
    unnamed x22 -> x20, local copies, waits for them, and re-layouts: 18.8 us -> 14.6 us
  transfers between devices with their start and end apart: 5 -> 5, of which waited for: 3 -> 4; matrix products, arithmetic and copies ran while one was open for 13% -> 7% of each run, Pallas kernels for 0% -> 0%
where the time goes in v1:
time: 592 us; the launch traced here: 588 us
  blocking collectives  209 us (35%)
  waiting for transfers between devices  196 us (33%)
  local copies, waits for them, and re-layouts  92.6 us (16%)
  starting transfers between devices  43.8 us (7%)
  matrix products  40.7 us (7%)
    all_gather x1, blocking collectives, body(): all_marks = lax.all_gather(marks, ('lat', 'lon'), axis=0, tiled=True)  153 us
    all_to_all x4, waiting for transfers between devices, all_by_exchange(): return jnp.concatenate(lax.all_to_all(sent, axis, 0, 0), axis=d)  148 us
    all_to_all x1, blocking collectives, body(): lax.all_to_all(blended.reshape(owned, owners, windows, inner), ('lat', 'l...  56.2 us
    all_to_all x1, waiting for transfers between devices, body(): lax.all_to_all(slots.reshape(owned, owners, windows, -1), ('lat', 'lon'),...  48 us
    all_to_all x4, starting transfers between devices, all_by_exchange(): return jnp.concatenate(lax.all_to_all(sent, axis, 0, 0), axis=d)  31.8 us
    dot_general x4, matrix products, product(): return jnp.dot(left_rows, right_rows, preferred_element_type=jnp.float32)  27.3 us
    another operation x2, local copies, waits for them, and re-layouts, attend(): split = proj.reshape(groups, rows, 3, HEADS, HD)  25.7 us
    unnamed x20, local copies, waits for them, and re-layouts  14.6 us
  transfers between devices with their start and end apart: 5, of which 4 were waited for; matrix products, arithmetic and copies ran while one was open for 7% of the time, Pallas kernels for 0%

profile of v1, /device:TPU:1, one launch (start us, length us, event | category | flops | bytes accessed | tf_op | source)
XLA Modules:
  0.0 588.0 jit_solution(9198732285463192850)
XLA Ops:
  0.0 1.1 constant_dynamic-slice_fusion.3
  1.1 1.4 stack.8
  2.5 8.6 %all-to-all-start = ((bf16[32,20,1280]{2,1,0:T(8,128)(2,1)}), bf16[32,20,1280]{2,1,0:T(8,128)(2,1)}, u32[]{:S(2)}, u32[]{:S(2)}) async-start(bf16[32,20,1280]{2,1,0:T(8,128)(2,1)} %stack.8), calls=%async_computation | async-start | bytes 3932160 | tf_op jit(solution)/shard_map/all_to_all | solution.py:14
  11.2 27.0 %all-to-all-done = bf16[32,20,1280]{2,1,0:T(8,128)(2,1)} async-done(((bf16[32,20,1280]{2,1,0:T(8,128)(2,1)}), bf16[32,20,1280]{2,1,0:T(8,128)(2,1)}, u32[]{:S(2)}, u32[]{:S(2)}) %all-to-all-start) | async-done | bytes 1638432 | tf_op jit(solution)/shard_map/all_to_all | solution.py:14
  38.2 4.4 stack.9
  42.6 6.4 %all-to-all-start.1 = ((bf16[32,40,3840]{2,1,0:T(8,128)(2,1)}), bf16[32,40,3840]{2,1,0:T(8,128)(2,1)}, u32[]{:S(2)}, u32[]{:S(2)}) async-start(bf16[32,40,3840]{2,1,0:T(8,128)(2,1)} %stack.9), calls=%async_computation.1 | async-start | bytes 19660800 | tf_op jit(solution)/shard_map/all_to_all | solution.py:14
  49.3 0.9 constant_dynamic-slice_fusion.1
  50.2 0.3 convolution_convert_fusion.6
  50.5 2.5 reshape.129
  53.0 113.6 %all-to-all-done.1 = bf16[32,40,3840]{2,1,0:T(8,128)(2,1)} async-done(((bf16[32,40,3840]{2,1,0:T(8,128)(2,1)}), bf16[32,40,3840]{2,1,0:T(8,128)(2,1)}, u32[]{:S(2)}, u32[]{:S(2)}) %all-to-all-start.1) | async-done | bytes 9830432 | tf_op jit(solution)/shard_map/all_to_all | solution.py:14
  166.6 1.9 stack.10
  168.5 12.0 %all-to-all-start.2 = ((bf16[32,40,1280]{2,1,0:T(8,128)(2,1)}), bf16[32,40,1280]{2,1,0:T(8,128)(2,1)}, u32[]{:S(2)}, u32[]{:S(2)}) async-start(bf16[32,40,1280]{2,1,0:T(8,128)(2,1)} %stack.10), calls=%async_computation.2 | async-start | bytes 6553600 | tf_op jit(solution)/shard_map/all_to_all | solution.py:14
  180.5 1.0 convert_reduce_fusion
  181.6 0.4 fusion.11
  182.0 9.3 %convolution_convert_fusion.1 = bf16[384,3840]{1,0:T(8,128)(2,1)} fusion(bf16[1280,3840]{1,0:T(8,128)(2,1)} %bitcast.2, bf16[384,1280]{1,0:T(8,128)(2,1)S(1)} %get-tuple-element.12, f32[384]{0:T(512)S(1)} %add_rsqrt_fusion.1, f32[384]{0:T(512)S(1)} %broadcast_multiply_fusion.1), kind=kOutput, calls=%fused_computation.7 | convolution fusion | flops 3778314240 | bytes 13765632 | tf_op jit(solution)/shard_map/dot_general | solution.py:24
  191.3 9.1 %reshape_reshape.12 = bf16[6,64,3,8,160]{4,3,2,1,0:T(8,128)(2,1)} reshape(bf16[384,3840]{1,0:T(8,128)(2,1)} %convolution_convert_fusion.1) | data formatting | bytes 5898240 | tf_op jit(solution)/shard_map/reshape;reshape | solution.py:35
  200.4 2.8 fusion.34
  203.2 0.8 multiply_select_fusion.4
  204.0 1.1 copy-done.6
  205.1 0.4 fusion.35
  205.5 3.9 fusion.21
  209.4 2.3 copy.51
  211.7 2.5 reshape_reshape.13
  214.2 7.2 %all-to-all-done.2 = bf16[32,40,1280]{2,1,0:T(8,128)(2,1)} async-done(((bf16[32,40,1280]{2,1,0:T(8,128)(2,1)}), bf16[32,40,1280]{2,1,0:T(8,128)(2,1)}, u32[]{:S(2)}, u32[]{:S(2)}) %all-to-all-start.2) | async-done | bytes 3276832 | tf_op jit(solution)/shard_map/all_to_all | solution.py:14
  221.5 3.8 fusion.36
  225.8 0.8 convolution_convert_fusion.2
  226.6 3.3 copy.52
  229.9 12.0 %all-to-all-start.3 = ((bf16[2,64,6,1280]{3,0,2,1:T(2,128)(2,1)}), bf16[2,64,6,1280]{3,0,2,1:T(2,128)(2,1)S(1)}, u32[]{:S(2)}, u32[]{:S(2)}) async-start(bf16[2,64,6,1280]{3,0,2,1:T(2,128)(2,1)} %copy.52), calls=%async_computation.3 | async-start | bytes 3932160 | tf_op jit(solution)/shard_map/all_to_all | solution.py:88
  241.9 1.0 constant_dynamic-slice_fusion
  242.9 48.0 %all-to-all-done.3 = bf16[2,64,6,1280]{3,0,2,1:T(2,128)(2,1)S(1)} async-done(((bf16[2,64,6,1280]{3,0,2,1:T(2,128)(2,1)}), bf16[2,64,6,1280]{3,0,2,1:T(2,128)(2,1)S(1)}, u32[]{:S(2)}, u32[]{:S(2)}) %all-to-all-start.3) | async-done | bytes 1966112 | tf_op jit(solution)/shard_map/all_to_all | solution.py:88
  290.9 4.4 stack.11
  295.3 4.8 all-to-all-start.4
  300.1 152.7 %all-gather = s32[64,6,64]{2,1,0:T(8,128)S(1)} all-gather(s32[1,6,64]{2,1,0:T(8,128)S(1)} %fusion.50), channel_id=1, replica_groups=mesh['batch'=4,'lat'=8,'lon'=8] {'lat','lon'}, dimensions={0}, use_global_device_ids=true | all-gather | bytes 99840 | tf_op jit(solution)/shard_map/all_gather | solution.py:63
  453.1 1.9 copy.53
  455.0 2.8 reshape.134
  457.7 13.2 %convolution_convert_fusion = bf16[768,3840]{1,0:T(8,128)(2,1)} fusion(bf16[768,1280]{1,0:T(8,128)(2,1)S(1)} %reshape.134, bf16[1280,3840]{1,0:T(8,128)(2,1)} %bitcast.11), kind=kOutput, calls=%fused_computation.6 | convolution fusion | flops 7552696320 | bytes 17694720 | tf_op jit(solution)/shard_map/dot_general | solution.py:24
  471.0 16.6 %reshape.140 = bf16[2,384,3,8,160]{4,3,2,1,0:T(8,128)(2,1)} reshape(bf16[768,3840]{1,0:T(8,128)(2,1)} %convolution_convert_fusion) | data formatting | bytes 11796480 | tf_op jit(solution)/shard_map/reshape;reshape | solution.py:35
  487.6 7.0 %fusion.33 = (bf16[2,384,1,8,160]{4,3,2,1,0:T(8,128)(2,1)}, bf16[2,384,1,8,160]{4,3,2,1,0:T(8,128)(2,1)}, bf16[2,384,1,8,160]{4,3,2,1,0:T(8,128)(2,1)}) fusion(bf16[2,384,3,8,160]{4,3,2,1,0:T(8,128)(2,1)} %reshape.140), kind=kLoop, calls=%fused_computation.64 | loop fusion | bytes 11796480 | tf_op jit(solution)/shard_map/slice | solution.py:44
  494.5 3.8 copy.70
  498.4 4.7 copy.71
  503.1 4.8 copy.69
  507.9 3.5 fusion.13
  511.3 4.1 fusion.37
  515.5 2.8 convert_bitcast_fusion
  518.2 5.0 copy.60
  523.2 6.9 %reshape_reshape.15 = bf16[2,64,6,1280]{3,0,2,1:T(2,128)(2,1)S(1)} reshape(bf16[2,384,8,160]{3,2,0,1:T(8,128)(2,1)} %copy.60) | data formatting | bytes 3932160 | tf_op jit(solution)/shard_map/reshape;reshape | solution.py:101
  530.1 56.2 %all_to_all.30 = bf16[2,64,6,1280]{3,0,2,1:T(2,128)(2,1)S(1)} all-to-all(bf16[2,64,6,1280]{3,0,2,1:T(2,128)(2,1)S(1)} %reshape_reshape.15), channel_id=1, replica_groups=mesh['batch'=4,'lat'=8,'lon'=8] {'lat','lon'}, dimensions={1} | all-to-all | bytes 3932160 | tf_op jit(solution)/shard_map/all_to_all | solution.py:100
  586.5 1.4 convolution_convert_fusion.3
  (32 shorter events, 1.5 us)
Async XLA Ops:
  0.0 11.1 %copy-start = (bf16[320,3840]{1,0:T(8,128)(2,1)S(1)}, bf16[320,3840]{1,0:T(8,128)(2,1)}, u32[]{:S(2)}) copy-start(bf16[320,3840]{1,0:T(8,128)(2,1)} %param.11) | copy-start | bytes 7372804
  2.5 35.7 %all-to-all-start = ((bf16[32,20,1280]{2,1,0:T(8,128)(2,1)}), bf16[32,20,1280]{2,1,0:T(8,128)(2,1)}, u32[]{:S(2)}, u32[]{:S(2)}) async-start(bf16[32,20,1280]{2,1,0:T(8,128)(2,1)} %stack.8), calls=%async_computation | async-start | bytes 3932160 | tf_op jit(solution)/shard_map/all_to_all | solution.py:14
  42.6 6.4 %copy-start.5 = (s32[1,2,3]{2,1,0:T(2,128)S(1)}, s32[1,2,3]{2,1,0:T(2,128)}, u32[]{:S(2)}) copy-start(s32[1,2,3]{2,1,0:T(2,128)} %param.9) | copy-start | bytes 76
  42.6 6.5 %copy-start.4 = (s32[1,2,3,64]{3,1,2,0:T(2,128)S(1)}, s32[1,2,3,64]{3,1,2,0:T(2,128)}, u32[]{:S(2)}) copy-start(s32[1,2,3,64]{3,1,2,0:T(2,128)} %param.8) | copy-start | bytes 4612
  42.6 7.6 %copy-start.3 = (bf16[1,2,3,128,640]{4,3,2,1,0:T(8,128)(2,1)S(1)}, bf16[1,2,3,128,640]{4,3,2,1,0:T(8,128)(2,1)}, u32[]{:S(2)}) copy-start(bf16[1,2,3,128,640]{4,3,2,1,0:T(8,128)(2,1)} %param.7) | copy-start | bytes 2949124
  42.6 124.0 %all-to-all-start.1 = ((bf16[32,40,3840]{2,1,0:T(8,128)(2,1)}), bf16[32,40,3840]{2,1,0:T(8,128)(2,1)}, u32[]{:S(2)}, u32[]{:S(2)}) async-start(bf16[32,40,3840]{2,1,0:T(8,128)(2,1)} %stack.9), calls=%async_computation.1 | async-start | bytes 19660800 | tf_op jit(solution)/shard_map/all_to_all | solution.py:14
  168.5 52.9 %all-to-all-start.2 = ((bf16[32,40,1280]{2,1,0:T(8,128)(2,1)}), bf16[32,40,1280]{2,1,0:T(8,128)(2,1)}, u32[]{:S(2)}, u32[]{:S(2)}) async-start(bf16[32,40,1280]{2,1,0:T(8,128)(2,1)} %stack.10), calls=%async_computation.2 | async-start | bytes 6553600 | tf_op jit(solution)/shard_map/all_to_all | solution.py:14
  203.9 1.2 copy-start.6
  229.9 60.9 %all-to-all-start.3 = ((bf16[2,64,6,1280]{3,0,2,1:T(2,128)(2,1)}), bf16[2,64,6,1280]{3,0,2,1:T(2,128)(2,1)S(1)}, u32[]{:S(2)}, u32[]{:S(2)}) async-start(bf16[2,64,6,1280]{3,0,2,1:T(2,128)(2,1)} %copy.52), calls=%async_computation.3 | async-start | bytes 3932160 | tf_op jit(solution)/shard_map/all_to_all | solution.py:88
  295.3 162.4 %all-to-all-start.4 = ((bf16[32,40,3840]{2,1,0:T(8,128)(2,1)}), bf16[32,40,3840]{2,1,0:T(8,128)(2,1)}, u32[]{:S(2)}, u32[]{:S(2)}) async-start(bf16[32,40,3840]{2,1,0:T(8,128)(2,1)} %stack.11), calls=%async_computation.4 | async-start | bytes 19660800 | tf_op jit(solution)/shard_map/all_to_all | solution.py:14
  511.3 4.1 copy-start.2
  586.3 1.7 copy-start.1
